TPU v7x, 512 devices: a whole 4x8x8 slice. The times are simulated.
512 devices in a mesh: space: 16 (over x, y_lo, core), term: 32 (over z, y_hi).
Axes of the slice: x: 4, y: 8 (y_hi: 4, y_lo: 2; y = y_hi * 2 + y_lo), z: 8, core: 2. Of those that a mesh axis runs over, the one named last changes fastest.
Arguments:
- right_modes: float32 [512, 64, 256], P(('space', 'term')), may hold values from -0.015625 to 0.015625
- adjoint_modes: float32 [512, 64, 256], P(('space', 'term')), may hold values from -6 to 6
- conductivity_terms: float32 [512, 256, 256], P('space', 'term'), may hold values from -6 to 6
Outputs:
- reduced_blocks: float32 [256, 4096], P('term', 'space')
All inputs are finite; a program needn't handle non-finite values.
Results may differ from a plain program's by a relative error of at most 0.000098.
Values sent between devices are 32-bit elements; how exact they have to be, the bound alone decides.
A program may use at most 64 MiB of HBM per device.

v0:
```python
import jax
import jax.numpy as jnp
from jax import lax
from jax.sharding import PartitionSpec as P

GY = 32


def extended(block, sides, width):
    for axis, dim in sides:
        count = lax.axis_size(axis)
        forward = [(i, i + 1) for i in range(count - 1)]
        backward = [(target, source) for source, target in forward]
        low = lax.ppermute(
            lax.slice_in_dim(block, block.shape[dim] - width, None, axis=dim), axis, forward
        )
        high = lax.ppermute(lax.slice_in_dim(block, 0, width, axis=dim), axis, backward)
        block = jnp.concatenate([low, block, high], axis=dim)
    return block


def shifted_cells(values, offset):
    zeros = jnp.zeros(values.shape[:-1] + (abs(offset),), jnp.float32)
    if offset > 0:
        return jnp.concatenate([values[..., offset:], zeros], axis=-1)
    return jnp.concatenate([zeros, values[..., :offset]], axis=-1)


def apply_terms(field_pad, coeff_pad, row_len):
    width = field_pad.shape[-1]
    column = jnp.arange(width) % row_len
    keep_next = (column != row_len - 1).astype(jnp.float32)
    keep_prev = (column != 0).astype(jnp.float32)
    centre = field_pad[None, 1:-1]
    coeff = coeff_pad[:, 1:-1, None, :]
    pairs = [
        (field_pad[None, 2:], coeff_pad[:, 2:, None, :]),
        (field_pad[None, :-2], coeff_pad[:, :-2, None, :]),
        (shifted_cells(centre, row_len), shifted_cells(coeff, row_len)),
        (shifted_cells(centre, -row_len), shifted_cells(coeff, -row_len)),
        (shifted_cells(centre, 1) * keep_next, shifted_cells(coeff, 1) * keep_next),
        (shifted_cells(centre, -1) * keep_prev, shifted_cells(coeff, -1) * keep_prev),
    ]
    result = jnp.zeros(coeff.shape[:2] + centre.shape[2:], jnp.float32)
    for other_field, other_coeff in pairs:
        result = result + 0.5 * (coeff + other_coeff) * (centre - other_field)
    return result


def assemble(field_pad, coeff_pad, adjoint, per_turn):
    modes = field_pad.shape[1]
    terms = coeff_pad.shape[1]
    ordered = jnp.moveaxis(coeff_pad, 1, 0)
    ordered = ordered.reshape((terms // per_turn, per_turn) + ordered.shape[1:])

    def one_block(coeff_block):
        image = apply_terms(field_pad, coeff_block, GY)
        return jnp.einsum("zrp,gzsp->grs", adjoint, image, precision=lax.Precision.HIGHEST)

    blocks = lax.map(one_block, ordered)
    return blocks.reshape(terms, modes * modes)


def local(right_modes, adjoint_modes, conductivity_terms):
    modes = right_modes.shape[1]
    slab_right, slab_adjoint = (
        lax.all_gather(right_modes, "term", axis=0, tiled=True),
        lax.all_gather(adjoint_modes, "term", axis=0, tiled=True),
    )
    stacked = jnp.concatenate([slab_right, conductivity_terms], axis=1)
    padded = extended(stacked, (("space", 0),), 1)
    partial_value = assemble(padded[:, :modes], padded[:, modes:], slab_adjoint, 1)
    return lax.psum_scatter(partial_value, "space", scatter_dimension=1, tiled=True)


def solution(mesh):
    placed = (
        P(("space", "term"), None, None),
        P(("space", "term"), None, None),
        P("space", "term", None),
    )
    return jax.shard_map(
        local, mesh=mesh, in_specs=placed, out_specs=P("term", "space"), check_vma=False
    )
```

profile of v0, /device:TPU:16, one launch (start us, length us, event | category | flops | bytes accessed | tf_op | source)
XLA Modules:
  0.0 315.2 jit_solution(1327591688766280557)
XLA Ops:
  6.5 0.7 all-gather.3.cloned.1.call-update
  7.3 0.7 all-gather.5.cloned.1.call-update
  8.1 93.2 %all-gather.3.cloned.1.call-done = f32[32,64,256]{2,1,0:T(8,128)} async-done(((f32[1,64,256]{2,1,0:T(8,128)}), f32[32,64,256]{2,1,0:T(8,128)}) %all-gather.3.cloned.1.call-update) | async-done | bytes 2097168 | tf_op jit(solution)/shard_map/all_gather | solution.py:67
  101.3 1.7 constant_dynamic-update-slice_fusion.2
  103.1 1.4 copy-done.3
  104.5 1.3 collective-permute-start.1
  105.8 3.0 collective-permute-start
  108.9 0.9 collective-permute-done
  109.7 1.0 maximum_bitcast_fusion
  111.0 1.3 copy-done.5
  112.3 2.5 fusion.38
  114.8 72.1 %all-gather.5.cloned.1.call-done = f32[32,64,256]{2,1,0:T(8,128)} async-done(((f32[1,64,256]{2,1,0:T(8,128)}), f32[32,64,256]{2,1,0:T(8,128)}) %all-gather.5.cloned.1.call-update) | async-done | bytes 2097168 | tf_op jit(solution)/shard_map/all_gather | solution.py:68
  186.9 58.4 %while.12 = (s32[]{:T(128)}, f32[8,1,64,64]{3,2,0,1:T(8,128)S(1)}, f32[8,1,34,256]{3,0,2,1:T(8,128)S(1)}, f32[32,64,256]{2,1,0:T(8,128)}, f32[32,64,256]{2,1,0:T...) while((s32[]{:T(128)}, f32[8,1,64,64]{3,2,0,1:T(8,128)S(1)}, ...), condition=%wide.region_1.2_spmd, body=%wide.region_0.1_spmd.sunk | while | flops 411683328 | bytes 63018424 | solution.py:60
  187.1 0.8 fusion.56
  187.9 0.8 fusion.57
  189.5 0.6 copy-done.1
  190.1 0.6 copy-done.2
  190.8 3.3 %fusion.61 = f32[1,1,64,64]{2,3,1,0:T(8,128)S(1)} fusion(f32[32,64,256]{2,1,0:T(8,128)S(1)} %copy-done.2, f32[32,64,256]{2,1,0:T(8,128)S(1)} %copy-done, f32[32,64,256]{2,1,0:T(8,128)S(1)} %copy-done.1, f32[1,32,64,255]{3,2,1,0:T(8,128)S(1)} %get-tuple-element.192, f32[1,32,64,255]{3,2,1,0:T(8,128)S(1)} %get-tuple-element.193, ...), kind=kOutput, calls=%fused_computation.24.clone.1 | convolution fusion | flops 411566080 | bytes 16992256 | tf_op jit(solution)/shard_map/while/body/eval_jaxpr/zrp,gzsp->grs/dot_general | solution.py:58
  194.4 0.8 fusion.56
  195.2 0.8 fusion.57
  197.4 0.6 copy-done.2
  198.1 3.3 %fusion.61 = f32[1,1,64,64]{2,3,1,0:T(8,128)S(1)} fusion(f32[32,64,256]{2,1,0:T(8,128)S(1)} %copy-done.2, f32[32,64,256]{2,1,0:T(8,128)S(1)} %copy-done, f32[32,64,256]{2,1,0:T(8,128)S(1)} %copy-done.1, f32[1,32,64,255]{3,2,1,0:T(8,128)S(1)} %get-tuple-element.192, f32[1,32,64,255]{3,2,1,0:T(8,128)S(1)} %get-tuple-element.193, ...), kind=kOutput, calls=%fused_computation.24.clone.1 | convolution fusion | flops 411566080 | bytes 16992256 | tf_op jit(solution)/shard_map/while/body/eval_jaxpr/zrp,gzsp->grs/dot_general | solution.py:58
  201.7 0.8 fusion.56
  202.5 0.8 fusion.57
  204.7 0.6 copy-done.2
  205.4 3.3 %fusion.61 = f32[1,1,64,64]{2,3,1,0:T(8,128)S(1)} fusion(f32[32,64,256]{2,1,0:T(8,128)S(1)} %copy-done.2, f32[32,64,256]{2,1,0:T(8,128)S(1)} %copy-done, f32[32,64,256]{2,1,0:T(8,128)S(1)} %copy-done.1, f32[1,32,64,255]{3,2,1,0:T(8,128)S(1)} %get-tuple-element.192, f32[1,32,64,255]{3,2,1,0:T(8,128)S(1)} %get-tuple-element.193, ...), kind=kOutput, calls=%fused_computation.24.clone.1 | convolution fusion | flops 411566080 | bytes 16992256 | tf_op jit(solution)/shard_map/while/body/eval_jaxpr/zrp,gzsp->grs/dot_general | solution.py:58
  209.0 0.8 fusion.56
  209.8 0.8 fusion.57
  212.0 0.6 copy-done.2
  212.7 3.3 %fusion.61 = f32[1,1,64,64]{2,3,1,0:T(8,128)S(1)} fusion(f32[32,64,256]{2,1,0:T(8,128)S(1)} %copy-done.2, f32[32,64,256]{2,1,0:T(8,128)S(1)} %copy-done, f32[32,64,256]{2,1,0:T(8,128)S(1)} %copy-done.1, f32[1,32,64,255]{3,2,1,0:T(8,128)S(1)} %get-tuple-element.192, f32[1,32,64,255]{3,2,1,0:T(8,128)S(1)} %get-tuple-element.193, ...), kind=kOutput, calls=%fused_computation.24.clone.1 | convolution fusion | flops 411566080 | bytes 16992256 | tf_op jit(solution)/shard_map/while/body/eval_jaxpr/zrp,gzsp->grs/dot_general | solution.py:58
  216.3 0.8 fusion.56
  217.1 0.8 fusion.57
  219.3 0.6 copy-done.2
  220.0 3.3 %fusion.61 = f32[1,1,64,64]{2,3,1,0:T(8,128)S(1)} fusion(f32[32,64,256]{2,1,0:T(8,128)S(1)} %copy-done.2, f32[32,64,256]{2,1,0:T(8,128)S(1)} %copy-done, f32[32,64,256]{2,1,0:T(8,128)S(1)} %copy-done.1, f32[1,32,64,255]{3,2,1,0:T(8,128)S(1)} %get-tuple-element.192, f32[1,32,64,255]{3,2,1,0:T(8,128)S(1)} %get-tuple-element.193, ...), kind=kOutput, calls=%fused_computation.24.clone.1 | convolution fusion | flops 411566080 | bytes 16992256 | tf_op jit(solution)/shard_map/while/body/eval_jaxpr/zrp,gzsp->grs/dot_general | solution.py:58
  223.6 0.8 fusion.56
  224.4 0.8 fusion.57
  226.6 0.6 copy-done.2
  227.3 3.3 %fusion.61 = f32[1,1,64,64]{2,3,1,0:T(8,128)S(1)} fusion(f32[32,64,256]{2,1,0:T(8,128)S(1)} %copy-done.2, f32[32,64,256]{2,1,0:T(8,128)S(1)} %copy-done, f32[32,64,256]{2,1,0:T(8,128)S(1)} %copy-done.1, f32[1,32,64,255]{3,2,1,0:T(8,128)S(1)} %get-tuple-element.192, f32[1,32,64,255]{3,2,1,0:T(8,128)S(1)} %get-tuple-element.193, ...), kind=kOutput, calls=%fused_computation.24.clone.1 | convolution fusion | flops 411566080 | bytes 16992256 | tf_op jit(solution)/shard_map/while/body/eval_jaxpr/zrp,gzsp->grs/dot_general | solution.py:58
  230.9 0.8 fusion.56
  231.7 0.8 fusion.57
  233.9 0.6 copy-done.2
  234.6 3.3 %fusion.61 = f32[1,1,64,64]{2,3,1,0:T(8,128)S(1)} fusion(f32[32,64,256]{2,1,0:T(8,128)S(1)} %copy-done.2, f32[32,64,256]{2,1,0:T(8,128)S(1)} %copy-done, f32[32,64,256]{2,1,0:T(8,128)S(1)} %copy-done.1, f32[1,32,64,255]{3,2,1,0:T(8,128)S(1)} %get-tuple-element.192, f32[1,32,64,255]{3,2,1,0:T(8,128)S(1)} %get-tuple-element.193, ...), kind=kOutput, calls=%fused_computation.24.clone.1 | convolution fusion | flops 411566080 | bytes 16992256 | tf_op jit(solution)/shard_map/while/body/eval_jaxpr/zrp,gzsp->grs/dot_general | solution.py:58
  238.2 0.8 fusion.56
  239.0 0.8 fusion.57
  241.2 0.6 copy-done.2
  241.9 3.3 %fusion.61 = f32[1,1,64,64]{2,3,1,0:T(8,128)S(1)} fusion(f32[32,64,256]{2,1,0:T(8,128)S(1)} %copy-done.2, f32[32,64,256]{2,1,0:T(8,128)S(1)} %copy-done, f32[32,64,256]{2,1,0:T(8,128)S(1)} %copy-done.1, f32[1,32,64,255]{3,2,1,0:T(8,128)S(1)} %get-tuple-element.192, f32[1,32,64,255]{3,2,1,0:T(8,128)S(1)} %get-tuple-element.193, ...), kind=kOutput, calls=%fused_computation.24.clone.1 | convolution fusion | flops 411566080 | bytes 16992256 | tf_op jit(solution)/shard_map/while/body/eval_jaxpr/zrp,gzsp->grs/dot_general | solution.py:58
  245.3 0.8 reshape.125
  246.1 62.6 %reduce-scatter.2.cloned.1.call-done = f32[8,256]{1,0:T(8,128)} async-done(((f32[8,4096]{1,0:T(8,128)}), f32[8,256]{1,0:T(8,128)}) %reduce-scatter.2.cloned.1.call-update) | async-done | bytes 8208 | tf_op jit(solution)/shard_map/reduce_scatter | solution.py:73
  (134 shorter events, 12.6 us)
Async XLA Ops:
  6.5 94.8 %all-gather.3.cloned.1.call-start = ((), (), s32[]{:S(2)}) async-start(), calls=%async_computation.1 | async-start | bytes 2162688 | tf_op jit(solution)/shard_map/all_gather | solution.py:67
  7.3 179.7 %all-gather.5.cloned.1.call-start = ((), (), s32[]{:S(2)}) async-start(), calls=%async_computation.2 | async-start | bytes 2162688 | tf_op jit(solution)/shard_map/all_gather | solution.py:68
  8.0 95.0 %copy-start.6 = (f32[32,8,256]{2,1,0:T(8,128)S(1)}, f32[32,8,256]{2,1,0:T(8,128)}, u32[]{:S(2)}) copy-start(f32[32,8,256]{2,1,0:T(8,128)} %param.7) | copy-start | bytes 786436
  8.0 300.7 %reduce-scatter.2.cloned.1.call-start = ((), (), s32[]{:S(2)}) async-start(), calls=%async_computation.3 | async-start | bytes 139264 | tf_op jit(solution)/shard_map/reduce_scatter | solution.py:73
  103.1 1.4 copy-start.3
  104.5 4.4 %collective-permute-start.1 = (f32[1,72,256]{2,1,0:T(8,128)S(1)}, f32[1,72,256]{2,1,0:T(8,128)S(1)}, u32[]{:S(2)}, u32[]{:S(2)}) collective-permute-start(f32[1,72,256]{2,1,0:T(8,128)S(1)} %get-tuple-element.131), channel_id=1, source_target_pairs={{32,0},{64,32},{96,64},{128,96},{160,128},{192,160},{224,192},{256... | collective-permute-start | bytes 221192 | tf_op jit(solution)/shard_map/ppermute | solution.py:17
  105.8 3.9 %collective-permute-start = (f32[1,72,256]{2,1,0:T(8,128)S(1)}, f32[1,72,256]{2,1,0:T(8,128)S(1)}, u32[]{:S(2)}, u32[]{:S(2)}) collective-permute-start(f32[1,72,256]{2,1,0:T(8,128)S(1)} %get-tuple-element.130), channel_id=1, source_target_pairs={{0,32},{32,64},{64,96},{96,128},{128,160},{160,192},{192,224},{224... | collective-permute-start | bytes 221192 | tf_op jit(solution)/shard_map/ppermute | solution.py:14
  108.9 1.9 copy-start.4
  110.7 1.6 copy-start.5
  187.9 1.6 copy-start
  187.9 2.2 copy-start.1
  187.9 2.8 copy-start.2
  195.2 1.6 copy-start
  195.2 2.2 copy-start.1
  195.2 2.8 copy-start.2
  202.5 1.6 copy-start
  202.5 2.2 copy-start.1
  202.5 2.8 copy-start.2
  209.8 1.6 copy-start
  209.8 2.2 copy-start.1
  209.8 2.8 copy-start.2
  217.1 1.6 copy-start
  217.1 2.2 copy-start.1
  217.1 2.8 copy-start.2
  224.4 1.6 copy-start
  224.4 2.2 copy-start.1
  224.4 2.8 copy-start.2
  231.7 1.6 copy-start
  231.7 2.2 copy-start.1
  231.7 2.8 copy-start.2
  239.0 1.6 copy-start
  239.0 2.2 copy-start.1
  239.0 2.8 copy-start.2
Sparse Core Ops, SparseCore 0:
  10.5 90.7 all-gather.2
  104.5 82.4 all-gather.4
  246.2 62.4 reduce-scatter.1
where the time goes:
time: 315 us
  waiting for transfers between devices  230 us (73%)
  local copies, waits for them, and re-layouts  35.1 us (11%)
  matrix products  26.7 us (8%)
  between operations  13.2 us (4%)
  other arithmetic  4.6 us (1%)
  starting transfers between devices  4.4 us (1%)
    all_gather x1, waiting for transfers between devices, local(): lax.all_gather(right_modes, 'term', axis=0, tiled=True)  93.2 us
    all_gather x1, waiting for transfers between devices, local(): lax.all_gather(adjoint_modes, 'term', axis=0, tiled=True)  72.1 us
    reduce_scatter x1, waiting for transfers between devices, local(): lax.psum_scatter(partial_value, 'space', scatter_dimension=1, tiled=True)  62.6 us
    dot_general x8, matrix products, one_block(): jnp.einsum('zrp,gzsp->grs', adjoint, image, precision=lax.Precision.HIGHEST)  26.7 us
    slice x32, local copies, waits for them, and re-layouts, shifted_cells(): return jnp.concatenate([values[..., offset:], zeros], axis=-1)  14 us
    while x48, local copies, waits for them, and re-layouts  13.6 us
  transfers between devices with their start and end apart: 5, of which 4 were waited for; matrix products, arithmetic and copies ran while one was open for 2% of the time, Pallas kernels for 0%

commit v1 on v0

--- a/solution.py
+++ b/solution.py
@@ -64,7 +64,9 @@
 def local(right_modes, adjoint_modes, conductivity_terms):
     modes = right_modes.shape[1]
     slab_right, slab_adjoint = (
-        lax.all_gather(right_modes, "term", axis=0, tiled=True),
+        jnp.concatenate(
+            lax.all_to_all(jnp.stack([right_modes] * lax.axis_size("term")), "term", 0, 0), axis=0
+        ),
         lax.all_gather(adjoint_modes, "term", axis=0, tiled=True),
     )
     stacked = jnp.concatenate([slab_right, conductivity_terms], axis=1)

time: 315 us -> 268 us (0.85)
  waiting for transfers between devices: 230 us -> 166 us
  starting transfers between devices: 4.4 us -> 20.6 us
    all_gather x1 -> x0, waiting for transfers between devices: 93.2 us -> none  [local(): lax.all_gather(right_modes, 'term', axis=0, tiled=True)]
    all_to_all x0 -> x1, waiting for transfers between devices: none -> 59.9 us  [local(): lax.all_to_all(jnp.stack([right_modes] * lax.axis_size('term')), 'term',...]
    all_gather x1, waiting for transfers between devices: 72.1 us -> 42.4 us  [local(): lax.all_gather(adjoint_modes, 'term', axis=0, tiled=True)]
    all_to_all x0 -> x1, starting transfers between devices: none -> 16.2 us  [local(): lax.all_to_all(jnp.stack([right_modes] * lax.axis_size('term')), 'term',...]
    unnamed x9 -> x6, local copies, waits for them, and re-layouts: 4.49 us -> 0.3 us
where the time goes in v1:
time: 268 us
  waiting for transfers between devices  166 us (62%)
  local copies, waits for them, and re-layouts  33.7 us (13%)
  matrix products  27.3 us (10%)
  starting transfers between devices  20.6 us (8%)
  between operations  13.5 us (5%)
  other arithmetic  5.39 us (2%)
    reduce_scatter x1, waiting for transfers between devices, local(): lax.psum_scatter(partial_value, 'space', scatter_dimension=1, tiled=True)  62.6 us
    all_to_all x1, waiting for transfers between devices, local(): lax.all_to_all(jnp.stack([right_modes] * lax.axis_size('term')), 'term',...  59.9 us
    all_gather x1, waiting for transfers between devices, local(): lax.all_gather(adjoint_modes, 'term', axis=0, tiled=True)  42.4 us
    dot_general x8, matrix products, one_block(): jnp.einsum('zrp,gzsp->grs', adjoint, image, precision=lax.Precision.HIGHEST)  27.3 us
    all_to_all x1, starting transfers between devices, local(): lax.all_to_all(jnp.stack([right_modes] * lax.axis_size('term')), 'term',...  16.2 us
    slice x32, local copies, waits for them, and re-layouts, shifted_cells(): return jnp.concatenate([values[..., offset:], zeros], axis=-1)  14 us
    while x48, local copies, waits for them, and re-layouts  13.6 us
  transfers between devices with their start and end apart: 5, of which 4 were waited for; matrix products, arithmetic and copies ran while one was open for 2% of the time, Pallas kernels for 0%

profile of v1, /device:TPU:16, one launch (start us, length us, event | category | flops | bytes accessed | tf_op | source)
XLA Modules:
  0.0 267.8 jit_solution(13044951956243058376)
XLA Ops:
  6.5 2.4 stack.2
  8.9 16.2 %all-to-all-start = ((f32[32,1,64,256]{3,2,1,0:T(8,128)}), f32[32,1,64,256]{3,2,1,0:T(8,128)S(1)}, u32[]{:S(2)}, u32[]{:S(2)}) async-start(f32[32,1,64,256]{3,2,1,0:T(8,128)} %stack.2), calls=%async_computation | async-start | bytes 4194304 | tf_op jit(solution)/shard_map/all_to_all | solution.py:68
  25.2 0.7 all-gather.2.cloned.1.call-update
  25.9 59.9 %all-to-all-done = f32[32,1,64,256]{3,2,1,0:T(8,128)S(1)} async-done(((f32[32,1,64,256]{3,2,1,0:T(8,128)}), f32[32,1,64,256]{3,2,1,0:T(8,128)S(1)}, u32[]{:S(2)}, u32[]{:S(2)}) %all-to-all-start) | async-done | bytes 2097184 | tf_op jit(solution)/shard_map/all_to_all | solution.py:68
  85.8 1.3 collective-permute-start.1
  87.1 3.0 %collective-permute-start = (f32[1,72,256]{2,1,0:T(8,128)S(1)}, f32[1,72,256]{2,1,0:T(8,128)S(1)}, u32[]{:S(2)}, u32[]{:S(2)}) collective-permute-start(f32[1,72,256]{2,1,0:T(8,128)S(1)} %get-tuple-element.130), channel_id=1, source_target_pairs={{0,32},{32,64},{64,96},{96,128},{128,160},{160,192},{192,224},{224... | collective-permute-start | bytes 221192 | tf_op jit(solution)/shard_map/ppermute | solution.py:14
  90.2 0.9 collective-permute-done
  91.1 1.9 pad_maximum_fusion
  93.3 2.5 fusion.38
  95.9 42.4 %all-gather.2.cloned.1.call-done = f32[32,64,256]{2,1,0:T(8,128)} async-done(((f32[1,64,256]{2,1,0:T(8,128)}), f32[32,64,256]{2,1,0:T(8,128)}) %all-gather.2.cloned.1.call-update) | async-done | bytes 2097168 | tf_op jit(solution)/shard_map/all_gather | solution.py:70
  138.2 59.3 %while.12 = (s32[]{:T(128)}, f32[8,1,64,64]{3,2,0,1:T(8,128)S(1)}, f32[8,1,34,256]{3,0,2,1:T(8,128)S(1)}, f32[32,64,256]{2,1,0:T(8,128)}, f32[32,64,256]{2,1,0:T...) while((s32[]{:T(128)}, f32[8,1,64,64]{3,2,0,1:T(8,128)S(1)}, ...), condition=%wide.region_1.2_spmd, body=%wide.region_0.1_spmd.sunk | while | flops 411683328 | bytes 63018424 | solution.py:60
  138.5 0.8 fusion.55
  139.3 0.8 fusion.56
  140.9 0.6 copy-done.1
  141.5 0.6 copy-done.2
  142.1 3.4 %fusion.60 = f32[1,1,64,64]{2,3,1,0:T(8,128)S(1)} fusion(f32[32,64,256]{2,1,0:T(8,128)S(1)} %copy-done.2, f32[32,64,256]{2,1,0:T(8,128)S(1)} %copy-done, f32[32,64,256]{2,1,0:T(8,128)S(1)} %copy-done.1, f32[1,32,64,255]{3,2,1,0:T(8,128)S(1)} %get-tuple-element.192, f32[1,32,64,255]{3,2,1,0:T(8,128)S(1)} %get-tuple-element.193, ...), kind=kOutput, calls=%fused_computation.24.clone.1 | convolution fusion | flops 411566080 | bytes 16992256 | tf_op jit(solution)/shard_map/while/body/eval_jaxpr/zrp,gzsp->grs/dot_general | solution.py:58
  145.9 0.8 fusion.55
  146.7 0.8 fusion.56
  148.3 0.6 copy-done.1
  148.9 0.6 copy-done.2
  149.6 3.4 %fusion.60 = f32[1,1,64,64]{2,3,1,0:T(8,128)S(1)} fusion(f32[32,64,256]{2,1,0:T(8,128)S(1)} %copy-done.2, f32[32,64,256]{2,1,0:T(8,128)S(1)} %copy-done, f32[32,64,256]{2,1,0:T(8,128)S(1)} %copy-done.1, f32[1,32,64,255]{3,2,1,0:T(8,128)S(1)} %get-tuple-element.192, f32[1,32,64,255]{3,2,1,0:T(8,128)S(1)} %get-tuple-element.193, ...), kind=kOutput, calls=%fused_computation.24.clone.1 | convolution fusion | flops 411566080 | bytes 16992256 | tf_op jit(solution)/shard_map/while/body/eval_jaxpr/zrp,gzsp->grs/dot_general | solution.py:58
  153.3 0.8 fusion.55
  154.1 0.8 fusion.56
  155.7 0.6 copy-done.1
  156.3 0.6 copy-done.2
  157.0 3.4 %fusion.60 = f32[1,1,64,64]{2,3,1,0:T(8,128)S(1)} fusion(f32[32,64,256]{2,1,0:T(8,128)S(1)} %copy-done.2, f32[32,64,256]{2,1,0:T(8,128)S(1)} %copy-done, f32[32,64,256]{2,1,0:T(8,128)S(1)} %copy-done.1, f32[1,32,64,255]{3,2,1,0:T(8,128)S(1)} %get-tuple-element.192, f32[1,32,64,255]{3,2,1,0:T(8,128)S(1)} %get-tuple-element.193, ...), kind=kOutput, calls=%fused_computation.24.clone.1 | convolution fusion | flops 411566080 | bytes 16992256 | tf_op jit(solution)/shard_map/while/body/eval_jaxpr/zrp,gzsp->grs/dot_general | solution.py:58
  160.7 0.8 fusion.55
  161.6 0.8 fusion.56
  163.8 0.6 copy-done.2
  164.4 3.4 %fusion.60 = f32[1,1,64,64]{2,3,1,0:T(8,128)S(1)} fusion(f32[32,64,256]{2,1,0:T(8,128)S(1)} %copy-done.2, f32[32,64,256]{2,1,0:T(8,128)S(1)} %copy-done, f32[32,64,256]{2,1,0:T(8,128)S(1)} %copy-done.1, f32[1,32,64,255]{3,2,1,0:T(8,128)S(1)} %get-tuple-element.192, f32[1,32,64,255]{3,2,1,0:T(8,128)S(1)} %get-tuple-element.193, ...), kind=kOutput, calls=%fused_computation.24.clone.1 | convolution fusion | flops 411566080 | bytes 16992256 | tf_op jit(solution)/shard_map/while/body/eval_jaxpr/zrp,gzsp->grs/dot_general | solution.py:58
  168.1 0.8 fusion.55
  169.0 0.8 fusion.56
  171.2 0.6 copy-done.2
  171.8 3.4 %fusion.60 = f32[1,1,64,64]{2,3,1,0:T(8,128)S(1)} fusion(f32[32,64,256]{2,1,0:T(8,128)S(1)} %copy-done.2, f32[32,64,256]{2,1,0:T(8,128)S(1)} %copy-done, f32[32,64,256]{2,1,0:T(8,128)S(1)} %copy-done.1, f32[1,32,64,255]{3,2,1,0:T(8,128)S(1)} %get-tuple-element.192, f32[1,32,64,255]{3,2,1,0:T(8,128)S(1)} %get-tuple-element.193, ...), kind=kOutput, calls=%fused_computation.24.clone.1 | convolution fusion | flops 411566080 | bytes 16992256 | tf_op jit(solution)/shard_map/while/body/eval_jaxpr/zrp,gzsp->grs/dot_general | solution.py:58
  175.6 0.8 fusion.55
  176.4 0.8 fusion.56
  178.6 0.6 copy-done.2
  179.2 3.4 %fusion.60 = f32[1,1,64,64]{2,3,1,0:T(8,128)S(1)} fusion(f32[32,64,256]{2,1,0:T(8,128)S(1)} %copy-done.2, f32[32,64,256]{2,1,0:T(8,128)S(1)} %copy-done, f32[32,64,256]{2,1,0:T(8,128)S(1)} %copy-done.1, f32[1,32,64,255]{3,2,1,0:T(8,128)S(1)} %get-tuple-element.192, f32[1,32,64,255]{3,2,1,0:T(8,128)S(1)} %get-tuple-element.193, ...), kind=kOutput, calls=%fused_computation.24.clone.1 | convolution fusion | flops 411566080 | bytes 16992256 | tf_op jit(solution)/shard_map/while/body/eval_jaxpr/zrp,gzsp->grs/dot_general | solution.py:58
  183.0 0.8 fusion.55
  183.8 0.8 fusion.56
  186.0 0.6 copy-done.2
  186.7 3.4 %fusion.60 = f32[1,1,64,64]{2,3,1,0:T(8,128)S(1)} fusion(f32[32,64,256]{2,1,0:T(8,128)S(1)} %copy-done.2, f32[32,64,256]{2,1,0:T(8,128)S(1)} %copy-done, f32[32,64,256]{2,1,0:T(8,128)S(1)} %copy-done.1, f32[1,32,64,255]{3,2,1,0:T(8,128)S(1)} %get-tuple-element.192, f32[1,32,64,255]{3,2,1,0:T(8,128)S(1)} %get-tuple-element.193, ...), kind=kOutput, calls=%fused_computation.24.clone.1 | convolution fusion | flops 411566080 | bytes 16992256 | tf_op jit(solution)/shard_map/while/body/eval_jaxpr/zrp,gzsp->grs/dot_general | solution.py:58
  190.4 0.8 fusion.55
  191.2 0.8 fusion.56
  193.4 0.6 copy-done.2
  194.1 3.4 %fusion.60 = f32[1,1,64,64]{2,3,1,0:T(8,128)S(1)} fusion(f32[32,64,256]{2,1,0:T(8,128)S(1)} %copy-done.2, f32[32,64,256]{2,1,0:T(8,128)S(1)} %copy-done, f32[32,64,256]{2,1,0:T(8,128)S(1)} %copy-done.1, f32[1,32,64,255]{3,2,1,0:T(8,128)S(1)} %get-tuple-element.192, f32[1,32,64,255]{3,2,1,0:T(8,128)S(1)} %get-tuple-element.193, ...), kind=kOutput, calls=%fused_computation.24.clone.1 | convolution fusion | flops 411566080 | bytes 16992256 | tf_op jit(solution)/shard_map/while/body/eval_jaxpr/zrp,gzsp->grs/dot_general | solution.py:58
  197.6 0.8 reshape.132
  198.4 62.6 %reduce-scatter.2.cloned.1.call-done = f32[8,256]{1,0:T(8,128)} async-done(((f32[8,4096]{1,0:T(8,128)}), f32[8,256]{1,0:T(8,128)}) %reduce-scatter.2.cloned.1.call-update) | async-done | bytes 8208 | tf_op jit(solution)/shard_map/reduce_scatter | solution.py:75
  (130 shorter events, 11.7 us)
Async XLA Ops:
  8.9 76.9 %copy-start.5 = (f32[32,8,256]{2,1,0:T(8,128)S(1)}, f32[32,8,256]{2,1,0:T(8,128)}, u32[]{:S(2)}) copy-start(f32[32,8,256]{2,1,0:T(8,128)} %param.7) | copy-start | bytes 786436
  8.9 76.9 %all-to-all-start = ((f32[32,1,64,256]{3,2,1,0:T(8,128)}), f32[32,1,64,256]{3,2,1,0:T(8,128)S(1)}, u32[]{:S(2)}, u32[]{:S(2)}) async-start(f32[32,1,64,256]{3,2,1,0:T(8,128)} %stack.2), calls=%async_computation | async-start | bytes 4194304 | tf_op jit(solution)/shard_map/all_to_all | solution.py:68
  25.1 113.1 %all-gather.2.cloned.1.call-start = ((), (), s32[]{:S(2)}) async-start(), calls=%async_computation.2 | async-start | bytes 2162688 | tf_op jit(solution)/shard_map/all_gather | solution.py:70
  25.8 235.1 %reduce-scatter.2.cloned.1.call-start = ((), (), s32[]{:S(2)}) async-start(), calls=%async_computation.3 | async-start | bytes 139264 | tf_op jit(solution)/shard_map/reduce_scatter | solution.py:75
  85.8 5.3 %copy-start.3 = (f32[32,1,64,256]{3,2,1,0:T(8,128)}, f32[32,1,64,256]{3,2,1,0:T(8,128)S(1)}, u32[]{:S(2)}) copy-start(f32[32,1,64,256]{3,2,1,0:T(8,128)S(1)} %all-to-all-done) | copy-start | bytes 6291460
  85.8 4.4 %collective-permute-start.1 = (f32[1,72,256]{2,1,0:T(8,128)S(1)}, f32[1,72,256]{2,1,0:T(8,128)S(1)}, u32[]{:S(2)}, u32[]{:S(2)}) collective-permute-start(f32[1,72,256]{2,1,0:T(8,128)S(1)} %get-tuple-element.131), channel_id=1, source_target_pairs={{32,0},{64,32},{96,64},{128,96},{160,128},{192,160},{224,192},{256... | collective-permute-start | bytes 221192 | tf_op jit(solution)/shard_map/ppermute | solution.py:17
  87.1 3.9 %collective-permute-start = (f32[1,72,256]{2,1,0:T(8,128)S(1)}, f32[1,72,256]{2,1,0:T(8,128)S(1)}, u32[]{:S(2)}, u32[]{:S(2)}) collective-permute-start(f32[1,72,256]{2,1,0:T(8,128)S(1)} %get-tuple-element.130), channel_id=1, source_target_pairs={{0,32},{32,64},{64,96},{96,128},{128,160},{160,192},{192,224},{224... | collective-permute-start | bytes 221192 | tf_op jit(solution)/shard_map/ppermute | solution.py:14
  91.1 2.2 copy-start.4
  139.3 1.6 copy-start
  139.3 2.2 copy-start.1
  139.3 2.8 %copy-start.2 = (f32[32,64,256]{2,1,0:T(8,128)S(1)}, f32[32,64,256]{2,1,0:T(8,128)}, u32[]{:S(2)}) copy-start(f32[32,64,256]{2,1,0:T(8,128)} %get-tuple-element.231) | copy-start | bytes 6291460 | tf_op jit(solution)/shard_map/while
  146.7 1.6 copy-start
  146.7 2.2 copy-start.1
  146.7 2.8 %copy-start.2 = (f32[32,64,256]{2,1,0:T(8,128)S(1)}, f32[32,64,256]{2,1,0:T(8,128)}, u32[]{:S(2)}) copy-start(f32[32,64,256]{2,1,0:T(8,128)} %get-tuple-element.231) | copy-start | bytes 6291460 | tf_op jit(solution)/shard_map/while
  154.1 1.6 copy-start
  154.1 2.2 copy-start.1
  154.1 2.8 %copy-start.2 = (f32[32,64,256]{2,1,0:T(8,128)S(1)}, f32[32,64,256]{2,1,0:T(8,128)}, u32[]{:S(2)}) copy-start(f32[32,64,256]{2,1,0:T(8,128)} %get-tuple-element.231) | copy-start | bytes 6291460 | tf_op jit(solution)/shard_map/while
  161.5 1.6 copy-start
  161.5 2.2 copy-start.1
  161.5 2.8 %copy-start.2 = (f32[32,64,256]{2,1,0:T(8,128)S(1)}, f32[32,64,256]{2,1,0:T(8,128)}, u32[]{:S(2)}) copy-start(f32[32,64,256]{2,1,0:T(8,128)} %get-tuple-element.231) | copy-start | bytes 6291460 | tf_op jit(solution)/shard_map/while
  168.9 1.6 copy-start
  169.0 2.2 copy-start.1
  169.0 2.8 %copy-start.2 = (f32[32,64,256]{2,1,0:T(8,128)S(1)}, f32[32,64,256]{2,1,0:T(8,128)}, u32[]{:S(2)}) copy-start(f32[32,64,256]{2,1,0:T(8,128)} %get-tuple-element.231) | copy-start | bytes 6291460 | tf_op jit(solution)/shard_map/while
  176.4 1.6 copy-start
  176.4 2.2 copy-start.1
  176.4 2.8 %copy-start.2 = (f32[32,64,256]{2,1,0:T(8,128)S(1)}, f32[32,64,256]{2,1,0:T(8,128)}, u32[]{:S(2)}) copy-start(f32[32,64,256]{2,1,0:T(8,128)} %get-tuple-element.231) | copy-start | bytes 6291460 | tf_op jit(solution)/shard_map/while
  183.8 1.6 copy-start
  183.8 2.2 copy-start.1
  183.8 2.8 %copy-start.2 = (f32[32,64,256]{2,1,0:T(8,128)S(1)}, f32[32,64,256]{2,1,0:T(8,128)}, u32[]{:S(2)}) copy-start(f32[32,64,256]{2,1,0:T(8,128)} %get-tuple-element.231) | copy-start | bytes 6291460 | tf_op jit(solution)/shard_map/while
  191.2 1.6 copy-start
  191.2 2.2 copy-start.1
  191.2 2.8 %copy-start.2 = (f32[32,64,256]{2,1,0:T(8,128)S(1)}, f32[32,64,256]{2,1,0:T(8,128)}, u32[]{:S(2)}) copy-start(f32[32,64,256]{2,1,0:T(8,128)} %get-tuple-element.231) | copy-start | bytes 6291460 | tf_op jit(solution)/shard_map/while
Sparse Core Ops, SparseCore 0:
  29.1 109.1 all-gather.1
  198.5 62.4 reduce-scatter.1
